TPU v7x, 32 devices: a whole 2x2x4 slice. The times are simulated.
32 devices in a mesh: view: 4 (over z), cell: 8 (over y, x, core).
Axes of the slice: x: 2, y: 2, z: 4, core: 2. Of those that a mesh axis runs over, the one named last changes fastest.
Arguments:
- params: float32 [59, 65536], P(None, 'cell'), may hold values from -6.22 to 3.2, as said below
- camera: float32 [4, 11], P('view'), may hold values from -0.3 to 1536, as said below
- targets: float32 [4, 256, 3, 256], P('view', 'cell'), may hold values from 0 to 1
- send_blocks: int32 [4, 8, 8, 16], P('view', 'cell'), may hold values from 0 to 255, as said below
- tile_blocks: int32 [4, 256, 16], P('view', 'cell'), may hold values from -1 to 127, as said below
- tile_order: int32 [4, 256, 512], P('view', 'cell'), may hold values from 0 to 511, as said below
Outputs:
- image: float32 [4, 256, 3, 256], P('view', 'cell')
- grads: float32 [59, 65536], P(None, 'cell')
Inputs may be any that keep to these rules, and one draw needn't show every extreme that they name: `params`: rows 0 to 2 lie in -3.2 to 3.2, rows 3 to 5 in log 0.002 to log 0.025, row 6 in 1 to 2, rows 7 to 9 in -1 to 1, row 10 in -3 to 2, rows 11 to 58 in -1.5 to 1.5. `camera`: quaternion first entry 1 to 2, its others -0.15 to 0.15, first two translation entries -0.3 to 0.3, third translation entry 4.5 to 6, focal lengths 2 to 3 times 16 max(32, 256 div 32), principal point within 20 of the image centre. `send_blocks`: the 16 numbers for one view, owner and receiving device are distinct. `tile_blocks`: A tile's live entries are distinct and come first, -1 fills the rest, and every tile has at least one live entry. `tile_order`: each tile's row is a permutation of 0 to 511.
All inputs are finite; a program needn't handle non-finite values.
Results may differ from a plain program's by a relative error of at most 0.0003.
Values sent between devices are 32-bit elements; how exact they have to be, the bound alone decides.
A program may use at most 128 MiB of HBM per device.

v0:
```python
import math
import jax
import jax.numpy as jnp
from jax import lax
from jax.sharding import PartitionSpec as P

BLOCK_GAUSSIANS = 32
TX = 32
HIGHEST_PRECISE = lax.Precision.HIGHEST
SH_ZERO = 0.28209479177387814
SH_ONE = 0.4886025119029199
SH_TWO = [
    1.0925484305920792,
    -1.0925484305920792,
    0.31539156525252005,
    -1.0925484305920792,
    0.5462742152960396,
]
SH_THREE = [
    -0.5900435899266435,
    2.890611442640554,
    -0.4570457994644658,
    0.3731763325901154,
    -0.4570457994644658,
    1.445305721320277,
    -0.5900435899266435,
]


def quat_matrix(qw, qx, qy, qz):
    return [
        [1.0 - 2.0 * (qy * qy + qz * qz), 2.0 * (qx * qy - qw * qz), 2.0 * (qx * qz + qw * qy)],
        [2.0 * (qx * qy + qw * qz), 1.0 - 2.0 * (qx * qx + qz * qz), 2.0 * (qy * qz - qw * qx)],
        [2.0 * (qx * qz - qw * qy), 2.0 * (qy * qz + qw * qx), 1.0 - 2.0 * (qx * qx + qy * qy)],
    ]


def sh_basis(dirx, diry, dirz):
    xx, yy, zz = (dirx * dirx, diry * diry, dirz * dirz)
    return [
        SH_ZERO + 0.0 * dirx,
        -SH_ONE * diry,
        SH_ONE * dirz,
        -SH_ONE * dirx,
        SH_TWO[0] * dirx * diry,
        SH_TWO[1] * diry * dirz,
        SH_TWO[2] * (2.0 * zz - xx - yy),
        SH_TWO[3] * dirx * dirz,
        SH_TWO[4] * (xx - yy),
        SH_THREE[0] * diry * (3.0 * xx - yy),
        SH_THREE[1] * dirx * diry * dirz,
        SH_THREE[2] * diry * (4.0 * zz - xx - yy),
        SH_THREE[3] * dirz * (2.0 * zz - 3.0 * xx - 3.0 * yy),
        SH_THREE[4] * dirx * (4.0 * zz - xx - yy),
        SH_THREE[5] * dirz * (xx - yy),
        SH_THREE[6] * dirx * (xx - 3.0 * yy),
    ]


def project(gauss, camera_row):
    cam_norm = jnp.sqrt(jnp.sum(camera_row[0:4] * camera_row[0:4]))
    cam_quat = camera_row[0:4] / cam_norm
    rotation = quat_matrix(cam_quat[0], cam_quat[1], cam_quat[2], cam_quat[3])
    focal_x, focal_y, centre_x, centre_y = (
        camera_row[7],
        camera_row[8],
        camera_row[9],
        camera_row[10],
    )
    cam_pos = [
        rotation[i][0] * gauss[0]
        + rotation[i][1] * gauss[1]
        + rotation[i][2] * gauss[2]
        + camera_row[4 + i]
        for i in range(3)
    ]
    inverse = 1.0 / cam_pos[2]
    screen_u = focal_x * cam_pos[0] * inverse + centre_x
    screen_w = focal_y * cam_pos[1] * inverse + centre_y
    gauss_norm = jnp.sqrt(
        gauss[6] * gauss[6] + gauss[7] * gauss[7] + gauss[8] * gauss[8] + gauss[9] * gauss[9]
    )
    grot = quat_matrix(
        gauss[6] / gauss_norm, gauss[7] / gauss_norm, gauss[8] / gauss_norm, gauss[9] / gauss_norm
    )
    scales = [jnp.exp(gauss[3 + k]) for k in range(3)]
    axes_cam = [
        [
            rotation[i][0] * grot[0][k] + rotation[i][1] * grot[1][k] + rotation[i][2] * grot[2][k]
            for k in range(3)
        ]
        for i in range(3)
    ]
    row_one = [
        (
            focal_x * inverse * axes_cam[0][k]
            - focal_x * cam_pos[0] * inverse * inverse * axes_cam[2][k]
        )
        * scales[k]
        for k in range(3)
    ]
    row_two = [
        (
            focal_y * inverse * axes_cam[1][k]
            - focal_y * cam_pos[1] * inverse * inverse * axes_cam[2][k]
        )
        * scales[k]
        for k in range(3)
    ]
    entry_a = row_one[0] * row_one[0] + row_one[1] * row_one[1] + row_one[2] * row_one[2] + 0.3
    entry_b = row_one[0] * row_two[0] + row_one[1] * row_two[1] + row_one[2] * row_two[2]
    entry_c = row_two[0] * row_two[0] + row_two[1] * row_two[1] + row_two[2] * row_two[2] + 0.3
    determinant = entry_a * entry_c - entry_b * entry_b
    opacity = jax.nn.sigmoid(gauss[10])
    distance = jnp.sqrt(cam_pos[0] * cam_pos[0] + cam_pos[1] * cam_pos[1] + cam_pos[2] * cam_pos[2])
    direction = [
        (rotation[0][j] * cam_pos[0] + rotation[1][j] * cam_pos[1] + rotation[2][j] * cam_pos[2])
        / distance
        for j in range(3)
    ]
    basis = sh_basis(direction[0], direction[1], direction[2])
    colors = []
    for channel in range(3):
        accum = 0.5 + basis[0] * gauss[11 + channel]
        for order in range(1, 16):
            accum = accum + basis[order] * gauss[11 + 3 * order + channel]
        colors.append(jnp.maximum(accum, 0.0))
    return jnp.stack(
        [
            screen_u,
            screen_w,
            entry_c / determinant,
            -entry_b / determinant,
            entry_a / determinant,
            opacity,
        ]
        + colors
    )


def expand(blocks, order):
    tiles_n, width = blocks.shape
    visible = blocks >= 0
    slots = jnp.maximum(blocks, 0)
    inner_product = jnp.arange(BLOCK_GAUSSIANS, dtype=jnp.int32)
    positions = (slots[:, :, None] * BLOCK_GAUSSIANS + inner_product).reshape(
        tiles_n, width * BLOCK_GAUSSIANS
    )
    visible = jnp.broadcast_to(visible[:, :, None], (tiles_n, width, BLOCK_GAUSSIANS)).reshape(
        tiles_n, width * BLOCK_GAUSSIANS
    )
    positions = jnp.take_along_axis(positions, order, axis=1)
    visible = jnp.take_along_axis(visible, order, axis=1)
    return (positions, visible)


def composite(fields, positions, visible, goal, first_tile):
    count, length = positions.shape
    pixels = goal.shape[-1]
    group = math.gcd(count, 4)
    steps_n = count // group
    pixel_ids = jnp.arange(pixels, dtype=jnp.int32)
    offset_x = (pixel_ids % 16).astype(jnp.float32) + 0.5
    offset_y = (pixel_ids // 16).astype(jnp.float32) + 0.5

    def step(carry, item):
        indices, alive, wanted, number = item
        tiles = first_tile + number * group + jnp.arange(group, dtype=jnp.int32)
        pix_x = (tiles % TX * 16).astype(jnp.float32)[:, None] + offset_x
        pix_y = (tiles // TX * 16).astype(jnp.float32)[:, None] + offset_y
        weights_mask = alive.astype(jnp.float32)

        def render(local_part):
            delta_x = pix_x[:, None, :] - local_part[0][:, :, None]
            delta_y = pix_y[:, None, :] - local_part[1][:, :, None]
            power = (
                -0.5
                * (
                    local_part[2][:, :, None] * delta_x * delta_x
                    + local_part[4][:, :, None] * delta_y * delta_y
                )
                - local_part[3][:, :, None] * delta_x * delta_y
            )
            alpha_value = (local_part[5] * weights_mask)[:, :, None] * jnp.exp(power)
            logs = jnp.log1p(-alpha_value)
            transmit_factor = jnp.exp(jnp.cumsum(logs, axis=1) - logs)
            return jnp.einsum(
                "dal,jda->djl",
                alpha_value * transmit_factor,
                local_part[6:9],
                precision=HIGHEST_PRECISE,
            )

        local_part = fields[:, indices]
        color, pullback = jax.vjp(render, local_part)
        local_grad = pullback((color - wanted) / pixels)[0]
        carry = carry.at[:, indices.reshape(-1)].add(local_grad.reshape(local_grad.shape[0], -1))
        return (carry, color)

    items = (
        positions.reshape(steps_n, group, length),
        visible.reshape(steps_n, group, length),
        goal.reshape(steps_n, group, 3, pixels),
        jnp.arange(steps_n, dtype=jnp.int32),
    )
    total, colors = lax.scan(step, jnp.zeros_like(fields), items)
    return (colors.reshape(count, 3, pixels), total)


def local(params, camera, targets, send_blocks, tile_blocks, tile_order):
    cells = lax.axis_size("cell")
    cell_index = lax.axis_index("cell")
    camera_row = camera[0]
    values_n = params.shape[0]
    owned_blocks = params.shape[1] // BLOCK_GAUSSIANS
    per_peer = send_blocks.shape[3]
    width = per_peer * BLOCK_GAUSSIANS
    picks = send_blocks[0, 0].reshape(-1)
    chosen = jnp.take(
        params.reshape(values_n, owned_blocks, BLOCK_GAUSSIANS), picks, axis=1
    ).reshape(values_n, cells * width)
    positions, visible = expand(tile_blocks[0], tile_order[0])
    first_tile = cell_index * tile_blocks.shape[1]
    received = lax.all_to_all(
        chosen.reshape(values_n, cells, width), "cell", split_axis=1, concat_axis=1, tiled=True
    ).reshape(values_n, cells * width)
    arrived, pullback = jax.vjp(lambda gathered: project(gathered, camera_row), received)
    picture, field_grad = composite(arrived, positions, visible, targets[0], first_tile)
    slot_grad = pullback(field_grad)[0]
    sent_grad = lax.all_to_all(
        slot_grad.reshape(values_n, cells, width), "cell", split_axis=1, concat_axis=1, tiled=True
    ).reshape(values_n, cells * width)
    per_block = jnp.transpose(
        sent_grad.reshape(values_n, cells * per_peer, BLOCK_GAUSSIANS), (1, 0, 2)
    )
    summed = jax.ops.segment_sum(per_block, picks, num_segments=owned_blocks)
    summed = jnp.transpose(summed, (1, 0, 2)).reshape(values_n, owned_blocks * BLOCK_GAUSSIANS)
    total = lax.psum(summed, "view")
    return (picture[None], total)


def solution(mesh):
    return jax.shard_map(
        local,
        mesh=mesh,
        in_specs=(
            P(None, "cell"),
            P("view", None),
            P("view", "cell", None, None),
            P("view", "cell", None, None),
            P("view", "cell", None),
            P("view", "cell", None),
        ),
        out_specs=(P("view", "cell", None, None), P(None, "cell")),
        check_vma=False,
    )
```

profile of v0, /device:TPU:0, one launch (start us, length us, event | category | flops | bytes accessed | tf_op | source)
XLA Modules:
  0.0 1059.9 jit_solution(7028042116414189610)
XLA Ops:
  20.5 5.2 all-to-all-start
  39.2 137.9 %gather_fusion.3 = pred[16384]{0:T(1024)(128)(4,1)S(1)} fusion(pred[32,512]{1,0:T(8,128)(4,1)S(1)} %reshape.6814, s32[16384]{0:T(1024)S(1)} %bitcast.267), kind=kCustom, calls=%fused_computation.3 | custom fusion | bytes 163840 | tf_op jit(solution)/shard_map/jit(take_along_axis)/gather | solution.py:153
  177.6 129.5 %gather_fusion.2 = s32[16384]{0:T(1024)S(1)} fusion(s32[32,512]{1,0:T(8,128)S(1)} %broadcast_add_fusion.4, s32[16384]{0:T(1024)S(1)} %bitcast.268), kind=kCustom, calls=%fused_computation.2 | custom fusion | bytes 262144 | tf_op jit(solution)/shard_map/jit(take_along_axis)/gather | solution.py:152
  331.4 563.3 %while.15 = (s32[]{:T(128)}, f32[9,4096]{0,1:T(8,128)}, f32[8,4,3,256]{3,2,1,0:T(4,128)}, s32[8,4,512]{2,1,0:T(4,128)}, f32[9,4096]{0,1:T(8,128)}, /*index=5*/pr...) while((s32[]{:T(128)}, f32[9,4096]{0,1:T(8,128)}, ...), condition=%wide.region_13.14_spmd.clone, body=%wide.region_1.13_spmd.clone.sunk | while | flops 240312416 | bytes 65026284 | solution.py:206
  346.5 7.0 gather_fusion
  371.0 6.0 fusion.186
  377.0 9.6 fusion.187
  391.6 7.6 fusion.188
  400.8 12.2 %scatter_fusion = f32[9,4096]{0,1:T(8,128)S(1)} fusion(f32[9,4096]{0,1:T(8,128)S(1)} %copy-done.2, s32[2048]{0:T(1024)S(1)} %bitcast.313, f32[2048,9]{1,0:T(8,128)S(1)} %copy.228), kind=kCustom, calls=%fused_computation.4.clone.clone.1 | custom fusion | flops 18432 | bytes 229376 | tf_op jit(solution)/shard_map/while/body/eval_jaxpr/scatter-add | solution.py:197
  415.1 7.0 gather_fusion
  427.0 4.7 fusion.184
  439.6 6.0 fusion.186
  445.6 9.6 fusion.187
  460.2 7.6 fusion.188
  469.4 12.2 %scatter_fusion = f32[9,4096]{0,1:T(8,128)S(1)} fusion(f32[9,4096]{0,1:T(8,128)S(1)} %copy-done.2, s32[2048]{0:T(1024)S(1)} %bitcast.313, f32[2048,9]{1,0:T(8,128)S(1)} %copy.228), kind=kCustom, calls=%fused_computation.4.clone.clone.1 | custom fusion | flops 18432 | bytes 229376 | tf_op jit(solution)/shard_map/while/body/eval_jaxpr/scatter-add | solution.py:197
  483.7 7.0 gather_fusion
  508.2 6.0 fusion.186
  514.3 9.6 fusion.187
  528.9 7.6 fusion.188
  538.0 12.2 %scatter_fusion = f32[9,4096]{0,1:T(8,128)S(1)} fusion(f32[9,4096]{0,1:T(8,128)S(1)} %copy-done.2, s32[2048]{0:T(1024)S(1)} %bitcast.313, f32[2048,9]{1,0:T(8,128)S(1)} %copy.228), kind=kCustom, calls=%fused_computation.4.clone.clone.1 | custom fusion | flops 18432 | bytes 229376 | tf_op jit(solution)/shard_map/while/body/eval_jaxpr/scatter-add | solution.py:197
  552.3 7.0 gather_fusion
  576.8 6.0 fusion.186
  582.8 9.6 fusion.187
  597.4 7.6 fusion.188
  606.6 12.2 %scatter_fusion = f32[9,4096]{0,1:T(8,128)S(1)} fusion(f32[9,4096]{0,1:T(8,128)S(1)} %copy-done.2, s32[2048]{0:T(1024)S(1)} %bitcast.313, f32[2048,9]{1,0:T(8,128)S(1)} %copy.228), kind=kCustom, calls=%fused_computation.4.clone.clone.1 | custom fusion | flops 18432 | bytes 229376 | tf_op jit(solution)/shard_map/while/body/eval_jaxpr/scatter-add | solution.py:197
  620.9 7.0 gather_fusion
  645.4 6.0 fusion.186
  651.4 9.6 fusion.187
  666.0 7.6 fusion.188
  675.2 12.2 %scatter_fusion = f32[9,4096]{0,1:T(8,128)S(1)} fusion(f32[9,4096]{0,1:T(8,128)S(1)} %copy-done.2, s32[2048]{0:T(1024)S(1)} %bitcast.313, f32[2048,9]{1,0:T(8,128)S(1)} %copy.228), kind=kCustom, calls=%fused_computation.4.clone.clone.1 | custom fusion | flops 18432 | bytes 229376 | tf_op jit(solution)/shard_map/while/body/eval_jaxpr/scatter-add | solution.py:197
  689.5 7.0 gather_fusion
  714.1 6.0 fusion.186
  720.1 9.6 fusion.187
  734.7 7.6 fusion.188
  743.9 12.2 %scatter_fusion = f32[9,4096]{0,1:T(8,128)S(1)} fusion(f32[9,4096]{0,1:T(8,128)S(1)} %copy-done.2, s32[2048]{0:T(1024)S(1)} %bitcast.313, f32[2048,9]{1,0:T(8,128)S(1)} %copy.228), kind=kCustom, calls=%fused_computation.4.clone.clone.1 | custom fusion | flops 18432 | bytes 229376 | tf_op jit(solution)/shard_map/while/body/eval_jaxpr/scatter-add | solution.py:197
  758.1 7.0 gather_fusion
  782.7 6.0 fusion.186
  788.7 9.6 fusion.187
  803.3 7.6 fusion.188
  812.5 12.2 %scatter_fusion = f32[9,4096]{0,1:T(8,128)S(1)} fusion(f32[9,4096]{0,1:T(8,128)S(1)} %copy-done.2, s32[2048]{0:T(1024)S(1)} %bitcast.313, f32[2048,9]{1,0:T(8,128)S(1)} %copy.228), kind=kCustom, calls=%fused_computation.4.clone.clone.1 | custom fusion | flops 18432 | bytes 229376 | tf_op jit(solution)/shard_map/while/body/eval_jaxpr/scatter-add | solution.py:197
  826.7 7.0 gather_fusion
  851.3 6.0 fusion.186
  857.3 9.6 fusion.187
  871.9 7.6 fusion.188
  881.1 12.2 %scatter_fusion = f32[9,4096]{0,1:T(8,128)S(1)} fusion(f32[9,4096]{0,1:T(8,128)S(1)} %copy-done.2, s32[2048]{0:T(1024)S(1)} %bitcast.313, f32[2048,9]{1,0:T(8,128)S(1)} %copy.228), kind=kCustom, calls=%fused_computation.4.clone.clone.1 | custom fusion | flops 18432 | bytes 229376 | tf_op jit(solution)/shard_map/while/body/eval_jaxpr/scatter-add | solution.py:197
  926.1 15.2 %all-to-all-done.1 = f32[59,8,512]{2,0,1:T(8,128)S(1)} async-done(((f32[59,8,512]{2,0,1:T(8,128)}), f32[59,8,512]{2,0,1:T(8,128)S(1)}, u32[]{:S(2)}, u32[]{:S(2)}) %all-to-all-start.1) | async-done | bytes 966688 | tf_op jit(solution)/shard_map/all_to_all | solution.py:230
  944.5 15.5 %scatter_fusion.1 = f32[256,59,32]{1,2,0:T(8,128)} fusion(f32[256,59,32]{1,2,0:T(8,128)} %broadcast_in_dim.76, s32[128]{0:T(128)S(1)} %reshape.6864, f32[128,59,32]{1,2,0:T(8,128)S(1)} %bitcast.272), kind=kCustom, calls=%fused_computation.5 | custom fusion | flops 241664 | bytes 2900480 | tf_op jit(solution)/shard_map/scatter-add | solution.py:236
  965.4 84.2 %all-reduce.78.cloned.1.call-done = f32[59,8192]{1,0:T(8,128)} async-done(((f32[59,8192]{1,0:T(8,128)}), f32[59,8192]{1,0:T(8,128)}) %all-reduce.78.cloned.1.call-update) | async-done | bytes 1933328 | tf_op jit(solution)/shard_map/psum | solution.py:238
  (977 shorter events, 276.9 us)
Async XLA Ops:
  17.3 8.4 copy-start.119
  17.3 8.5 copy-start.120
  17.3 9.8 copy-start.52
  20.5 289.3 %all-to-all-start = ((f32[59,8,512]{2,0,1:T(8,128)}), f32[59,8,512]{2,0,1:T(8,128)S(1)}, u32[]{:S(2)}, u32[]{:S(2)}) async-start(f32[59,8,512]{2,0,1:T(8,128)} %copy.134), calls=%async_computation | async-start | bytes 2097152 | tf_op jit(solution)/shard_map/all_to_all | solution.py:224
  177.6 129.5 %copy-start.117 = (f32[1,32,3,256]{3,1,2,0:T(8,128)S(1)}, f32[1,32,3,256]{3,1,2,0:T(8,128)}, u32[]{:S(2)}) copy-start(f32[1,32,3,256]{3,1,2,0:T(8,128)} %param.10) | copy-start | bytes 294916
  310.7 9.8 copy-start.53
  310.7 9.8 copy-start.55
  310.7 9.8 copy-start.57
  310.7 9.8 copy-start.59
  310.7 15.4 %copy-start.28 = (f32[1,8,512]{2,0,1:T(1,128)}, f32[1,8,512]{2,0,1:T(1,128)S(1)}, u32[]{:S(2)}) copy-start(f32[1,8,512]{2,0,1:T(1,128)S(1)} %get-tuple-element.415) | copy-start | bytes 49156
  312.3 10.5 copy-start.14
  313.6 9.1 copy-start.12
  313.6 12.6 %copy-start.50 = (f32[1,8,512]{2,0,1:T(1,128)}, f32[1,8,512]{2,0,1:T(1,128)S(1)}, u32[]{:S(2)}) copy-start(f32[1,8,512]{2,0,1:T(1,128)S(1)} %get-tuple-element.416) | copy-start | bytes 49156
  391.6 7.7 copy-start.31
  894.8 12.6 %copy-start.40 = (f32[1,4096]{1,0:T(1,128)S(1)}, f32[1,4096]{1,0:T(1,128)}, u32[]{:S(2)}) copy-start(f32[1,4096]{1,0:T(1,128)} %get-tuple-element.302) | copy-start | bytes 49156
  894.8 13.4 %copy-start.33 = (f32[1,4096]{1,0:T(1,128)S(1)}, f32[1,4096]{1,0:T(1,128)}, u32[]{:S(2)}) copy-start(f32[1,4096]{1,0:T(1,128)} %copy-done.32) | copy-start | bytes 49156
  894.8 13.4 %copy-start.35 = (f32[1,4096]{1,0:T(1,128)S(1)}, f32[1,4096]{1,0:T(1,128)}, u32[]{:S(2)}) copy-start(f32[1,4096]{1,0:T(1,128)} %copy-done.34) | copy-start | bytes 49156
  894.8 13.4 %copy-start.37 = (f32[1,4096]{1,0:T(1,128)S(1)}, f32[1,4096]{1,0:T(1,128)}, u32[]{:S(2)}) copy-start(f32[1,4096]{1,0:T(1,128)} %copy-done.36) | copy-start | bytes 49156
  894.8 13.4 %copy-start.39 = (f32[1,4096]{1,0:T(1,128)S(1)}, f32[1,4096]{1,0:T(1,128)}, u32[]{:S(2)}) copy-start(f32[1,4096]{1,0:T(1,128)} %copy-done.38) | copy-start | bytes 49156
  894.8 13.4 %copy-start.45 = (f32[1,4096]{1,0:T(1,128)S(1)}, f32[1,4096]{1,0:T(1,128)}, u32[]{:S(2)}) copy-start(f32[1,4096]{1,0:T(1,128)} %copy-done.44) | copy-start | bytes 49156
  894.8 13.4 %copy-start.47 = (f32[1,4096]{1,0:T(1,128)S(1)}, f32[1,4096]{1,0:T(1,128)}, u32[]{:S(2)}) copy-start(f32[1,4096]{1,0:T(1,128)} %copy-done.46) | copy-start | bytes 49156
  894.9 13.4 %copy-start.49 = (f32[1,4096]{1,0:T(1,128)S(1)}, f32[1,4096]{1,0:T(1,128)}, u32[]{:S(2)}) copy-start(f32[1,4096]{1,0:T(1,128)} %copy-done.48) | copy-start | bytes 49156
  897.1 12.8 %copy-start.41 = (f32[1,4096]{1,0:T(1,128)S(1)}, f32[1,4096]{1,0:T(1,128)}, u32[]{:S(2)}) copy-start(f32[1,4096]{1,0:T(1,128)} %get-tuple-element.321) | copy-start | bytes 49156
  897.1 12.8 %copy-start.42 = (f32[1,4096]{1,0:T(1,128)S(1)}, f32[1,4096]{1,0:T(1,128)}, u32[]{:S(2)}) copy-start(f32[1,4096]{1,0:T(1,128)} %get-tuple-element.327) | copy-start | bytes 49156
  897.1 12.8 %copy-start.43 = (f32[1,4096]{1,0:T(1,128)S(1)}, f32[1,4096]{1,0:T(1,128)}, u32[]{:S(2)}) copy-start(f32[1,4096]{1,0:T(1,128)} %get-tuple-element.333) | copy-start | bytes 49156
  897.2 12.8 %copy-start.51 = (f32[1,8,512]{2,0,1:T(1,128)S(1)}, f32[1,8,512]{2,0,1:T(1,128)}, u32[]{:S(2)}) copy-start(f32[1,8,512]{2,0,1:T(1,128)} %copy-done.50) | copy-start | bytes 49156
  897.2 12.8 %copy-start.70 = (f32[1,8,512]{2,0,1:T(1,128)S(1)}, f32[1,8,512]{2,0,1:T(1,128)}, u32[]{:S(2)}) copy-start(f32[1,8,512]{2,0,1:T(1,128)} %copy-done.69) | copy-start | bytes 49156
  897.2 12.8 %copy-start.72 = (f32[1,8,512]{2,0,1:T(1,128)S(1)}, f32[1,8,512]{2,0,1:T(1,128)}, u32[]{:S(2)}) copy-start(f32[1,8,512]{2,0,1:T(1,128)} %copy-done.71) | copy-start | bytes 49156
  897.2 12.8 %copy-start.74 = (f32[1,8,512]{2,0,1:T(1,128)S(1)}, f32[1,8,512]{2,0,1:T(1,128)}, u32[]{:S(2)}) copy-start(f32[1,8,512]{2,0,1:T(1,128)} %copy-done.73) | copy-start | bytes 49156
  897.2 12.8 %copy-start.76 = (f32[1,8,512]{2,0,1:T(1,128)S(1)}, f32[1,8,512]{2,0,1:T(1,128)}, u32[]{:S(2)}) copy-start(f32[1,8,512]{2,0,1:T(1,128)} %copy-done.75) | copy-start | bytes 49156
  897.2 12.8 %copy-start.78 = (f32[1,8,512]{2,0,1:T(1,128)S(1)}, f32[1,8,512]{2,0,1:T(1,128)}, u32[]{:S(2)}) copy-start(f32[1,8,512]{2,0,1:T(1,128)} %copy-done.77) | copy-start | bytes 49156
  897.2 12.8 %copy-start.80 = (f32[1,8,512]{2,0,1:T(1,128)S(1)}, f32[1,8,512]{2,0,1:T(1,128)}, u32[]{:S(2)}) copy-start(f32[1,8,512]{2,0,1:T(1,128)} %copy-done.79) | copy-start | bytes 49156
  897.2 12.8 %copy-start.82 = (f32[1,8,512]{2,0,1:T(1,128)S(1)}, f32[1,8,512]{2,0,1:T(1,128)}, u32[]{:S(2)}) copy-start(f32[1,8,512]{2,0,1:T(1,128)} %copy-done.81) | copy-start | bytes 49156
  897.2 12.8 %copy-start.84 = (f32[1,8,512]{2,0,1:T(1,128)S(1)}, f32[1,8,512]{2,0,1:T(1,128)}, u32[]{:S(2)}) copy-start(f32[1,8,512]{2,0,1:T(1,128)} %copy-done.83) | copy-start | bytes 49156
  897.2 12.8 %copy-start.86 = (f32[1,8,512]{2,0,1:T(1,128)S(1)}, f32[1,8,512]{2,0,1:T(1,128)}, u32[]{:S(2)}) copy-start(f32[1,8,512]{2,0,1:T(1,128)} %copy-done.85) | copy-start | bytes 49156
  897.3 12.8 %copy-start.88 = (f32[1,8,512]{2,0,1:T(1,128)S(1)}, f32[1,8,512]{2,0,1:T(1,128)}, u32[]{:S(2)}) copy-start(f32[1,8,512]{2,0,1:T(1,128)} %copy-done.87) | copy-start | bytes 49156
  897.3 12.8 %copy-start.90 = (f32[1,8,512]{2,0,1:T(1,128)S(1)}, f32[1,8,512]{2,0,1:T(1,128)}, u32[]{:S(2)}) copy-start(f32[1,8,512]{2,0,1:T(1,128)} %copy-done.89) | copy-start | bytes 49156
  897.3 12.8 %copy-start.92 = (f32[1,8,512]{2,0,1:T(1,128)S(1)}, f32[1,8,512]{2,0,1:T(1,128)}, u32[]{:S(2)}) copy-start(f32[1,8,512]{2,0,1:T(1,128)} %copy-done.91) | copy-start | bytes 49156
  897.3 12.8 %copy-start.94 = (f32[1,8,512]{2,0,1:T(1,128)S(1)}, f32[1,8,512]{2,0,1:T(1,128)}, u32[]{:S(2)}) copy-start(f32[1,8,512]{2,0,1:T(1,128)} %copy-done.93) | copy-start | bytes 49156
  898.4 9.9 copy-start.100
  898.4 11.7 %copy-start.96 = (f32[1,8,512]{2,0,1:T(1,128)S(1)}, f32[1,8,512]{2,0,1:T(1,128)}, u32[]{:S(2)}) copy-start(f32[1,8,512]{2,0,1:T(1,128)} %copy-done.95) | copy-start | bytes 49156
  898.4 11.7 %copy-start.98 = (f32[1,8,512]{2,0,1:T(1,128)S(1)}, f32[1,8,512]{2,0,1:T(1,128)}, u32[]{:S(2)}) copy-start(f32[1,8,512]{2,0,1:T(1,128)} %copy-done.97) | copy-start | bytes 49156
  898.4 11.7 %copy-start.101 = (f32[1,4096]{1,0:T(1,128)S(1)}, f32[1,4096]{1,0:T(1,128)}, u32[]{:S(2)}) copy-start(f32[1,4096]{1,0:T(1,128)} %get-tuple-element.297) | copy-start | bytes 49156
  899.4 10.8 %copy-start.102 = (f32[1,4096]{1,0:T(1,128)S(1)}, f32[1,4096]{1,0:T(1,128)}, u32[]{:S(2)}) copy-start(f32[1,4096]{1,0:T(1,128)} %get-tuple-element.300) | copy-start | bytes 49156
  900.4 9.8 copy-start.103
  900.4 9.8 copy-start.105
  921.7 19.6 %all-to-all-start.1 = ((f32[59,8,512]{2,0,1:T(8,128)}), f32[59,8,512]{2,0,1:T(8,128)S(1)}, u32[]{:S(2)}, u32[]{:S(2)}) async-start(f32[59,8,512]{2,0,1:T(8,128)} %copy.150), calls=%async_computation.1 | async-start | bytes 2097152 | tf_op jit(solution)/shard_map/all_to_all | solution.py:230
  925.9 123.6 %all-reduce.78.cloned.1.call-start = ((), (), s32[]{:S(2)}) async-start(), calls=%async_computation.2 | async-start | bytes 4194304 | tf_op jit(solution)/shard_map/psum | solution.py:238
  (202 other events, 555.3 us)
Sparse Core Ops, SparseCore 0:
  964.0 85.5 all-reduce.77
where the time goes:
time: 1070 us; the launch traced here: 1060 us
  local copies, waits for them, and re-layouts  444 us (41%)
  other arithmetic  374 us (35%)
  waiting for transfers between devices  99.4 us (9%)
  matrix products  82.1 us (8%)
  between operations  27.9 us (3%)
  loops' own time  23 us (2%)
    gather x2, local copies, waits for them, and re-layouts, expand(): visible = jnp.take_along_axis(visible, order, axis=1)  138 us
    another operation x48, other arithmetic  134 us
    gather x2, local copies, waits for them, and re-layouts, expand(): positions = jnp.take_along_axis(positions, order, axis=1)  129 us
    scatter-add x8, other arithmetic, step(): carry.at[:, indices.reshape(-1)]  97.8 us
    psum x1, waiting for transfers between devices, local(): total = lax.psum(summed, 'view')  84.2 us
    dot_general x24, matrix products, render(): jnp.einsum('dal,jda->djl', alpha_value * transmit_factor, local_part[6:9]...  82.1 us
    reduce_sum x8, other arithmetic, render(): local_part[3][:, :, None] * delta_x * delta_y  60.7 us
    gather x16, local copies, waits for them, and re-layouts, step(): local_part = fields[:, indices]  59 us
  transfers between devices with their start and end apart: 3, of which 2 were waited for; matrix products, arithmetic and copies ran while one was open for 26% of the time, Pallas kernels for 0%

commit v1 on v0

--- a/solution.py
+++ b/solution.py
@@ -235,7 +235,7 @@
     )
     summed = jax.ops.segment_sum(per_block, picks, num_segments=owned_blocks)
     summed = jnp.transpose(summed, (1, 0, 2)).reshape(values_n, owned_blocks * BLOCK_GAUSSIANS)
-    total = lax.psum(summed, "view")
+    total = lax.all_gather(summed, "view").sum(axis=0)
     return (picture[None], total)
 
 

time: 1070 us -> 1140 us (1.065)
  waiting for transfers between devices: 99.4 us -> 163 us
    all_gather x0 -> x1, waiting for transfers between devices: none -> 148 us  [local(): total = lax.all_gather(summed, 'view').sum(axis=0)]
    psum x1 -> x0, waiting for transfers between devices: 84.2 us -> none  [local(): total = lax.psum(summed, 'view')]
  transfers between devices with their start and end apart: 3 -> 3, of which waited for: 2 -> 2; matrix products, arithmetic and copies ran while one was open for 26% -> 24% of each run, Pallas kernels for 0% -> 0%
where the time goes in v1:
time: 1140 us; the launch traced here: 1130 us
  local copies, waits for them, and re-layouts  442 us (39%)
  other arithmetic  378 us (33%)
  waiting for transfers between devices  163 us (14%)
  matrix products  82.1 us (7%)
  between operations  28.2 us (2%)
  loops' own time  23.4 us (2%)
    all_gather x1, waiting for transfers between devices, local(): total = lax.all_gather(summed, 'view').sum(axis=0)  148 us
    gather x2, local copies, waits for them, and re-layouts, expand(): visible = jnp.take_along_axis(visible, order, axis=1)  138 us
    another operation x48, other arithmetic  134 us
    gather x2, local copies, waits for them, and re-layouts, expand(): positions = jnp.take_along_axis(positions, order, axis=1)  129 us
    scatter-add x8, other arithmetic, step(): carry.at[:, indices.reshape(-1)]  97.8 us
    dot_general x24, matrix products, render(): jnp.einsum('dal,jda->djl', alpha_value * transmit_factor, local_part[6:9]...  82.1 us
    reduce_sum x8, other arithmetic, render(): local_part[3][:, :, None] * delta_x * delta_y  60.7 us
    gather x16, local copies, waits for them, and re-layouts, step(): local_part = fields[:, indices]  59 us
  transfers between devices with their start and end apart: 3, of which 2 were waited for; matrix products, arithmetic and copies ran while one was open for 24% of the time, Pallas kernels for 0%

profile of v1, /device:TPU:0, one launch (start us, length us, event | category | flops | bytes accessed | tf_op | source)
XLA Modules:
  0.0 1126.7 jit_solution(16010438619425450748)
XLA Ops:
  20.5 5.2 all-to-all-start
  39.5 137.9 %gather_fusion.3 = pred[16384]{0:T(1024)(128)(4,1)S(1)} fusion(pred[32,512]{1,0:T(8,128)(4,1)S(1)} %reshape.6811, s32[16384]{0:T(1024)S(1)} %bitcast.267), kind=kCustom, calls=%fused_computation.3 | custom fusion | bytes 163840 | tf_op jit(solution)/shard_map/jit(take_along_axis)/gather | solution.py:153
  177.9 129.5 %gather_fusion.2 = s32[16384]{0:T(1024)S(1)} fusion(s32[32,512]{1,0:T(8,128)S(1)} %broadcast_add_fusion.4, s32[16384]{0:T(1024)S(1)} %bitcast.268), kind=kCustom, calls=%fused_computation.2 | custom fusion | bytes 262144 | tf_op jit(solution)/shard_map/jit(take_along_axis)/gather | solution.py:152
  331.5 564.7 %while.15 = (s32[]{:T(128)}, f32[9,4096]{0,1:T(8,128)}, f32[8,4,3,256]{3,2,1,0:T(4,128)}, s32[8,4,512]{2,1,0:T(4,128)}, f32[9,4096]{0,1:T(8,128)}, /*index=5*/pr...) while((s32[]{:T(128)}, f32[9,4096]{0,1:T(8,128)}, ...), condition=%wide.region_13.14_spmd.clone, body=%wide.region_1.13_spmd.clone.sunk | while | flops 240312416 | bytes 65026284 | solution.py:206
  346.5 7.0 gather_fusion
  371.3 6.0 fusion.186
  377.3 9.6 fusion.187
  391.9 7.6 fusion.188
  401.1 12.2 %scatter_fusion = f32[9,4096]{0,1:T(8,128)S(1)} fusion(f32[9,4096]{0,1:T(8,128)S(1)} %copy-done.2, s32[2048]{0:T(1024)S(1)} %bitcast.313, f32[2048,9]{1,0:T(8,128)S(1)} %copy.233), kind=kCustom, calls=%fused_computation.4.clone.clone.1 | custom fusion | flops 18432 | bytes 229376 | tf_op jit(solution)/shard_map/while/body/eval_jaxpr/scatter-add | solution.py:197
  415.3 7.0 gather_fusion
  440.0 6.0 fusion.186
  446.0 9.6 fusion.187
  460.7 7.6 fusion.188
  469.9 12.2 %scatter_fusion = f32[9,4096]{0,1:T(8,128)S(1)} fusion(f32[9,4096]{0,1:T(8,128)S(1)} %copy-done.2, s32[2048]{0:T(1024)S(1)} %bitcast.313, f32[2048,9]{1,0:T(8,128)S(1)} %copy.233), kind=kCustom, calls=%fused_computation.4.clone.clone.1 | custom fusion | flops 18432 | bytes 229376 | tf_op jit(solution)/shard_map/while/body/eval_jaxpr/scatter-add | solution.py:197
  484.1 7.0 gather_fusion
  508.8 6.0 fusion.186
  514.8 9.6 fusion.187
  529.5 7.6 fusion.188
  538.6 12.2 %scatter_fusion = f32[9,4096]{0,1:T(8,128)S(1)} fusion(f32[9,4096]{0,1:T(8,128)S(1)} %copy-done.2, s32[2048]{0:T(1024)S(1)} %bitcast.313, f32[2048,9]{1,0:T(8,128)S(1)} %copy.233), kind=kCustom, calls=%fused_computation.4.clone.clone.1 | custom fusion | flops 18432 | bytes 229376 | tf_op jit(solution)/shard_map/while/body/eval_jaxpr/scatter-add | solution.py:197
  552.9 7.0 gather_fusion
  577.6 6.0 fusion.186
  583.6 9.6 fusion.187
  598.2 7.6 fusion.188
  607.4 12.2 %scatter_fusion = f32[9,4096]{0,1:T(8,128)S(1)} fusion(f32[9,4096]{0,1:T(8,128)S(1)} %copy-done.2, s32[2048]{0:T(1024)S(1)} %bitcast.313, f32[2048,9]{1,0:T(8,128)S(1)} %copy.233), kind=kCustom, calls=%fused_computation.4.clone.clone.1 | custom fusion | flops 18432 | bytes 229376 | tf_op jit(solution)/shard_map/while/body/eval_jaxpr/scatter-add | solution.py:197
  621.7 7.0 gather_fusion
  646.4 6.0 fusion.186
  652.4 9.6 fusion.187
  667.0 7.6 fusion.188
  676.2 12.2 %scatter_fusion = f32[9,4096]{0,1:T(8,128)S(1)} fusion(f32[9,4096]{0,1:T(8,128)S(1)} %copy-done.2, s32[2048]{0:T(1024)S(1)} %bitcast.313, f32[2048,9]{1,0:T(8,128)S(1)} %copy.233), kind=kCustom, calls=%fused_computation.4.clone.clone.1 | custom fusion | flops 18432 | bytes 229376 | tf_op jit(solution)/shard_map/while/body/eval_jaxpr/scatter-add | solution.py:197
  690.5 7.0 gather_fusion
  715.2 6.0 fusion.186
  721.2 9.6 fusion.187
  735.8 7.6 fusion.188
  745.0 12.2 %scatter_fusion = f32[9,4096]{0,1:T(8,128)S(1)} fusion(f32[9,4096]{0,1:T(8,128)S(1)} %copy-done.2, s32[2048]{0:T(1024)S(1)} %bitcast.313, f32[2048,9]{1,0:T(8,128)S(1)} %copy.233), kind=kCustom, calls=%fused_computation.4.clone.clone.1 | custom fusion | flops 18432 | bytes 229376 | tf_op jit(solution)/shard_map/while/body/eval_jaxpr/scatter-add | solution.py:197
  759.3 7.0 gather_fusion
  784.0 6.0 fusion.186
  790.0 9.6 fusion.187
  804.6 7.6 fusion.188
  813.8 12.2 %scatter_fusion = f32[9,4096]{0,1:T(8,128)S(1)} fusion(f32[9,4096]{0,1:T(8,128)S(1)} %copy-done.2, s32[2048]{0:T(1024)S(1)} %bitcast.313, f32[2048,9]{1,0:T(8,128)S(1)} %copy.233), kind=kCustom, calls=%fused_computation.4.clone.clone.1 | custom fusion | flops 18432 | bytes 229376 | tf_op jit(solution)/shard_map/while/body/eval_jaxpr/scatter-add | solution.py:197
  828.1 7.0 gather_fusion
  852.8 6.0 fusion.186
  858.8 9.6 fusion.187
  873.4 7.6 fusion.188
  882.6 12.2 %scatter_fusion = f32[9,4096]{0,1:T(8,128)S(1)} fusion(f32[9,4096]{0,1:T(8,128)S(1)} %copy-done.2, s32[2048]{0:T(1024)S(1)} %bitcast.313, f32[2048,9]{1,0:T(8,128)S(1)} %copy.233), kind=kCustom, calls=%fused_computation.4.clone.clone.1 | custom fusion | flops 18432 | bytes 229376 | tf_op jit(solution)/shard_map/while/body/eval_jaxpr/scatter-add | solution.py:197
  927.0 15.2 %all-to-all-done.1 = f32[59,8,512]{2,0,1:T(8,128)S(1)} async-done(((f32[59,8,512]{2,0,1:T(8,128)}), f32[59,8,512]{2,0,1:T(8,128)S(1)}, u32[]{:S(2)}, u32[]{:S(2)}) %all-to-all-start.1) | async-done | bytes 966688 | tf_op jit(solution)/shard_map/all_to_all | solution.py:230
  945.4 15.5 %scatter_fusion.1 = f32[256,59,32]{1,2,0:T(8,128)} fusion(f32[256,59,32]{1,2,0:T(8,128)} %broadcast_in_dim.76, s32[128]{0:T(128)S(1)} %reshape.6860, f32[128,59,32]{1,2,0:T(8,128)S(1)} %bitcast.272), kind=kCustom, calls=%fused_computation.5 | custom fusion | flops 241664 | bytes 2900480 | tf_op jit(solution)/shard_map/scatter-add | solution.py:236
  966.4 147.6 %all-gather.2.cloned.1.call-done = f32[4,59,8192]{2,1,0:T(8,128)} async-done(((f32[1,59,8192]{2,1,0:T(8,128)}), f32[4,59,8192]{2,1,0:T(8,128)}) %all-gather.2.cloned.1.call-update) | async-done | bytes 7733264 | tf_op jit(solution)/shard_map/all_gather | solution.py:238
  1114.0 5.5 reduce_sum.117
  (977 shorter events, 278.7 us)
Async XLA Ops:
  17.3 8.4 copy-start.119
  17.3 8.5 copy-start.120
  17.3 9.8 copy-start.52
  20.5 289.6 %all-to-all-start = ((f32[59,8,512]{2,0,1:T(8,128)}), f32[59,8,512]{2,0,1:T(8,128)S(1)}, u32[]{:S(2)}, u32[]{:S(2)}) async-start(f32[59,8,512]{2,0,1:T(8,128)} %copy.136), calls=%async_computation | async-start | bytes 2097152 | tf_op jit(solution)/shard_map/all_to_all | solution.py:224
  177.9 129.5 %copy-start.117 = (f32[1,32,3,256]{3,1,2,0:T(8,128)S(1)}, f32[1,32,3,256]{3,1,2,0:T(8,128)}, u32[]{:S(2)}) copy-start(f32[1,32,3,256]{3,1,2,0:T(8,128)} %param.10) | copy-start | bytes 294916
  311.0 9.6 copy-start.53
  311.0 9.6 copy-start.55
  311.0 9.6 copy-start.57
  311.0 9.6 copy-start.59
  311.0 15.2 %copy-start.28 = (f32[1,8,512]{2,0,1:T(1,128)}, f32[1,8,512]{2,0,1:T(1,128)S(1)}, u32[]{:S(2)}) copy-start(f32[1,8,512]{2,0,1:T(1,128)S(1)} %get-tuple-element.421) | copy-start | bytes 49156
  312.5 10.4 copy-start.14
  313.8 8.9 copy-start.12
  313.8 12.4 %copy-start.50 = (f32[1,8,512]{2,0,1:T(1,128)}, f32[1,8,512]{2,0,1:T(1,128)S(1)}, u32[]{:S(2)}) copy-start(f32[1,8,512]{2,0,1:T(1,128)S(1)} %get-tuple-element.422) | copy-start | bytes 49156
  529.5 7.7 copy-start.31
  896.3 12.2 %copy-start.40 = (f32[1,4096]{1,0:T(1,128)S(1)}, f32[1,4096]{1,0:T(1,128)}, u32[]{:S(2)}) copy-start(f32[1,4096]{1,0:T(1,128)} %get-tuple-element.308) | copy-start | bytes 49156
  896.3 13.0 %copy-start.33 = (f32[1,4096]{1,0:T(1,128)S(1)}, f32[1,4096]{1,0:T(1,128)}, u32[]{:S(2)}) copy-start(f32[1,4096]{1,0:T(1,128)} %copy-done.32) | copy-start | bytes 49156
  896.3 13.0 %copy-start.35 = (f32[1,4096]{1,0:T(1,128)S(1)}, f32[1,4096]{1,0:T(1,128)}, u32[]{:S(2)}) copy-start(f32[1,4096]{1,0:T(1,128)} %copy-done.34) | copy-start | bytes 49156
  896.3 13.0 %copy-start.37 = (f32[1,4096]{1,0:T(1,128)S(1)}, f32[1,4096]{1,0:T(1,128)}, u32[]{:S(2)}) copy-start(f32[1,4096]{1,0:T(1,128)} %copy-done.36) | copy-start | bytes 49156
  896.3 13.0 %copy-start.39 = (f32[1,4096]{1,0:T(1,128)S(1)}, f32[1,4096]{1,0:T(1,128)}, u32[]{:S(2)}) copy-start(f32[1,4096]{1,0:T(1,128)} %copy-done.38) | copy-start | bytes 49156
  896.3 13.0 %copy-start.45 = (f32[1,4096]{1,0:T(1,128)S(1)}, f32[1,4096]{1,0:T(1,128)}, u32[]{:S(2)}) copy-start(f32[1,4096]{1,0:T(1,128)} %copy-done.44) | copy-start | bytes 49156
  896.3 13.0 %copy-start.47 = (f32[1,4096]{1,0:T(1,128)S(1)}, f32[1,4096]{1,0:T(1,128)}, u32[]{:S(2)}) copy-start(f32[1,4096]{1,0:T(1,128)} %copy-done.46) | copy-start | bytes 49156
  896.4 13.0 %copy-start.49 = (f32[1,4096]{1,0:T(1,128)S(1)}, f32[1,4096]{1,0:T(1,128)}, u32[]{:S(2)}) copy-start(f32[1,4096]{1,0:T(1,128)} %copy-done.48) | copy-start | bytes 49156
  898.6 12.4 %copy-start.41 = (f32[1,4096]{1,0:T(1,128)S(1)}, f32[1,4096]{1,0:T(1,128)}, u32[]{:S(2)}) copy-start(f32[1,4096]{1,0:T(1,128)} %get-tuple-element.327) | copy-start | bytes 49156
  898.6 12.4 %copy-start.42 = (f32[1,4096]{1,0:T(1,128)S(1)}, f32[1,4096]{1,0:T(1,128)}, u32[]{:S(2)}) copy-start(f32[1,4096]{1,0:T(1,128)} %get-tuple-element.333) | copy-start | bytes 49156
  898.6 12.4 %copy-start.43 = (f32[1,4096]{1,0:T(1,128)S(1)}, f32[1,4096]{1,0:T(1,128)}, u32[]{:S(2)}) copy-start(f32[1,4096]{1,0:T(1,128)} %get-tuple-element.339) | copy-start | bytes 49156
  898.7 12.4 %copy-start.51 = (f32[1,8,512]{2,0,1:T(1,128)S(1)}, f32[1,8,512]{2,0,1:T(1,128)}, u32[]{:S(2)}) copy-start(f32[1,8,512]{2,0,1:T(1,128)} %copy-done.50) | copy-start | bytes 49156
  898.7 12.4 %copy-start.70 = (f32[1,8,512]{2,0,1:T(1,128)S(1)}, f32[1,8,512]{2,0,1:T(1,128)}, u32[]{:S(2)}) copy-start(f32[1,8,512]{2,0,1:T(1,128)} %copy-done.69) | copy-start | bytes 49156
  898.7 12.4 %copy-start.72 = (f32[1,8,512]{2,0,1:T(1,128)S(1)}, f32[1,8,512]{2,0,1:T(1,128)}, u32[]{:S(2)}) copy-start(f32[1,8,512]{2,0,1:T(1,128)} %copy-done.71) | copy-start | bytes 49156
  898.7 12.4 %copy-start.74 = (f32[1,8,512]{2,0,1:T(1,128)S(1)}, f32[1,8,512]{2,0,1:T(1,128)}, u32[]{:S(2)}) copy-start(f32[1,8,512]{2,0,1:T(1,128)} %copy-done.73) | copy-start | bytes 49156
  898.7 12.4 %copy-start.76 = (f32[1,8,512]{2,0,1:T(1,128)S(1)}, f32[1,8,512]{2,0,1:T(1,128)}, u32[]{:S(2)}) copy-start(f32[1,8,512]{2,0,1:T(1,128)} %copy-done.75) | copy-start | bytes 49156
  898.7 12.4 %copy-start.78 = (f32[1,8,512]{2,0,1:T(1,128)S(1)}, f32[1,8,512]{2,0,1:T(1,128)}, u32[]{:S(2)}) copy-start(f32[1,8,512]{2,0,1:T(1,128)} %copy-done.77) | copy-start | bytes 49156
  898.7 12.4 %copy-start.80 = (f32[1,8,512]{2,0,1:T(1,128)S(1)}, f32[1,8,512]{2,0,1:T(1,128)}, u32[]{:S(2)}) copy-start(f32[1,8,512]{2,0,1:T(1,128)} %copy-done.79) | copy-start | bytes 49156
  898.7 12.4 %copy-start.82 = (f32[1,8,512]{2,0,1:T(1,128)S(1)}, f32[1,8,512]{2,0,1:T(1,128)}, u32[]{:S(2)}) copy-start(f32[1,8,512]{2,0,1:T(1,128)} %copy-done.81) | copy-start | bytes 49156
  898.7 12.4 %copy-start.84 = (f32[1,8,512]{2,0,1:T(1,128)S(1)}, f32[1,8,512]{2,0,1:T(1,128)}, u32[]{:S(2)}) copy-start(f32[1,8,512]{2,0,1:T(1,128)} %copy-done.83) | copy-start | bytes 49156
  898.7 12.4 %copy-start.86 = (f32[1,8,512]{2,0,1:T(1,128)S(1)}, f32[1,8,512]{2,0,1:T(1,128)}, u32[]{:S(2)}) copy-start(f32[1,8,512]{2,0,1:T(1,128)} %copy-done.85) | copy-start | bytes 49156
  898.8 12.4 %copy-start.88 = (f32[1,8,512]{2,0,1:T(1,128)S(1)}, f32[1,8,512]{2,0,1:T(1,128)}, u32[]{:S(2)}) copy-start(f32[1,8,512]{2,0,1:T(1,128)} %copy-done.87) | copy-start | bytes 49156
  898.8 12.4 %copy-start.90 = (f32[1,8,512]{2,0,1:T(1,128)S(1)}, f32[1,8,512]{2,0,1:T(1,128)}, u32[]{:S(2)}) copy-start(f32[1,8,512]{2,0,1:T(1,128)} %copy-done.89) | copy-start | bytes 49156
  898.8 12.4 %copy-start.92 = (f32[1,8,512]{2,0,1:T(1,128)S(1)}, f32[1,8,512]{2,0,1:T(1,128)}, u32[]{:S(2)}) copy-start(f32[1,8,512]{2,0,1:T(1,128)} %copy-done.91) | copy-start | bytes 49156
  898.8 12.4 %copy-start.94 = (f32[1,8,512]{2,0,1:T(1,128)S(1)}, f32[1,8,512]{2,0,1:T(1,128)}, u32[]{:S(2)}) copy-start(f32[1,8,512]{2,0,1:T(1,128)} %copy-done.93) | copy-start | bytes 49156
  899.9 9.5 copy-start.100
  899.9 11.4 %copy-start.96 = (f32[1,8,512]{2,0,1:T(1,128)S(1)}, f32[1,8,512]{2,0,1:T(1,128)}, u32[]{:S(2)}) copy-start(f32[1,8,512]{2,0,1:T(1,128)} %copy-done.95) | copy-start | bytes 49156
  899.9 11.4 %copy-start.98 = (f32[1,8,512]{2,0,1:T(1,128)S(1)}, f32[1,8,512]{2,0,1:T(1,128)}, u32[]{:S(2)}) copy-start(f32[1,8,512]{2,0,1:T(1,128)} %copy-done.97) | copy-start | bytes 49156
  899.9 11.4 %copy-start.101 = (f32[1,4096]{1,0:T(1,128)S(1)}, f32[1,4096]{1,0:T(1,128)}, u32[]{:S(2)}) copy-start(f32[1,4096]{1,0:T(1,128)} %get-tuple-element.303) | copy-start | bytes 49156
  900.9 10.4 copy-start.102
  901.9 9.4 copy-start.103
  901.9 9.4 copy-start.105
  922.7 19.6 %all-to-all-start.1 = ((f32[59,8,512]{2,0,1:T(8,128)}), f32[59,8,512]{2,0,1:T(8,128)S(1)}, u32[]{:S(2)}, u32[]{:S(2)}) async-start(f32[59,8,512]{2,0,1:T(8,128)} %copy.152), calls=%async_computation.1 | async-start | bytes 2097152 | tf_op jit(solution)/shard_map/all_to_all | solution.py:230
  926.9 187.1 %all-gather.2.cloned.1.call-start = ((), (), s32[]{:S(2)}) async-start(), calls=%async_computation.2 | async-start | bytes 10485760 | tf_op jit(solution)/shard_map/all_gather | solution.py:238
  (202 other events, 557.6 us)
Sparse Core Ops, SparseCore 0:
  964.9 148.9 all-gather.1
